TPU v7x, 32 devices: a whole 2x2x4 slice. The times are simulated.
32 devices in a mesh: replica: 16 (over z, y, x), dom: 2 (over core).
Axes of the slice: x: 2, y: 2, z: 4, core: 2. Of those that a mesh axis runs over, the one named last changes fastest.
Arguments:
- inputs: bfloat16 [2, 384, 8192], P(None, 'replica', 'dom'), may hold values from -6 to 6
- targets: bfloat16 [2, 384, 8192], P(None, 'replica', 'dom'), may hold values from -0.8984375 to 0.8984375
- w_first: float32 [8192, 8192], P('replica', 'dom'), may hold values from -5 to 5
- acc_first: float32 [8192, 8192], P('replica', 'dom'), may hold values from 0.5 to 8
- w_second: float32 [8192, 8192], P('dom', 'replica'), may hold values from -5 to 5
- acc_second: float32 [8192, 8192], P('dom', 'replica'), may hold values from 0.5 to 8
Outputs:
- new_first: float32 [8192, 8192], P('replica', 'dom')
- new_acc_first: float32 [8192, 8192], P('replica', 'dom')
- new_second: float32 [8192, 8192], P('dom', 'replica')
- new_acc_second: float32 [8192, 8192], P('dom', 'replica')
All inputs are finite; a program needn't handle non-finite values.
Results may differ from a plain program's by a relative error of at most 0.015.
Values may be sent and summed in bfloat16 or wider, within the bound.
No kernel may reach another device: no remote copies, remote signals or barrier semaphores. Data moves between devices by JAX's collectives and lax.ppermute only.
A program may use at most 192 MiB of HBM per device.

v0:
```python
import math
import jax
import jax.numpy as jnp
from jax import lax
from jax.sharding import PartitionSpec as P

learn_rate = 0.05
error_weight = 0.25


def local(inputs, targets, w_first, acc_first, w_second, acc_second):
    full_width = w_first.shape[1] * lax.axis_size("dom")
    unit_scale = 1.0 / math.sqrt(0.4 * full_width)
    for round_index in range(inputs.shape[0]):
        first_half = w_first.astype(jnp.bfloat16)
        second_half = w_second.astype(jnp.bfloat16)
        round_batch = lax.all_gather(inputs[round_index], "replica", axis=0, tiled=True)
        goal_rows = targets[round_index]
        first_terms = (
            lax.dot_general(
                round_batch,
                first_half,
                (((1,), (1,)), ((), ())),
                preferred_element_type=jnp.float32,
            )
            * unit_scale
        )
        first_out = jnp.tanh(lax.psum(first_terms.astype(jnp.bfloat16), "dom").astype(jnp.float32))
        first_rows = first_out.astype(jnp.bfloat16)
        second_out = jnp.tanh(
            lax.psum_scatter(
                lax.dot_general(
                    first_rows,
                    second_half,
                    (((1,), (1,)), ((), ())),
                    preferred_element_type=jnp.float32,
                )
                * unit_scale,
                "replica",
                scatter_dimension=0,
                tiled=True,
            )
        )
        error_own = (
            (second_out - goal_rows.astype(jnp.float32))
            * error_weight
            * (1.0 - second_out * second_out)
        ).astype(jnp.bfloat16)
        error_half = lax.all_gather(error_own, "replica", axis=0, tiled=True)
        second_grad = lax.dot_general(
            error_half, first_rows, (((0,), (0,)), ((), ())), preferred_element_type=jnp.float32
        )
        back_terms = (
            jnp.dot(error_half, second_half, preferred_element_type=jnp.float32) * unit_scale
        )
        back_pre = lax.psum(back_terms.astype(jnp.bfloat16), "dom").astype(jnp.float32)
        first_error = (back_pre * (1.0 - first_out * first_out)).astype(jnp.bfloat16)
        first_grad = lax.dot_general(
            first_error, round_batch, (((0,), (0,)), ((), ())), preferred_element_type=jnp.float32
        )
        acc_first = acc_first + first_grad * first_grad
        w_first = w_first - learn_rate * first_grad / jnp.sqrt(acc_first)
        acc_second = acc_second + second_grad * second_grad
        w_second = w_second - learn_rate * second_grad / jnp.sqrt(acc_second)
    return (w_first, acc_first, w_second, acc_second)


def solution(mesh):
    placed = (
        P(None, "replica", "dom"),
        P(None, "replica", "dom"),
        P("replica", "dom"),
        P("replica", "dom"),
        P("dom", "replica"),
        P("dom", "replica"),
    )
    return jax.shard_map(
        local,
        mesh=mesh,
        in_specs=placed,
        out_specs=(
            P("replica", "dom"),
            P("replica", "dom"),
            P("dom", "replica"),
            P("dom", "replica"),
        ),
        check_vma=False,
    )
```

profile of v0, /device:TPU:0, one launch (start us, length us, event | category | flops | bytes accessed | tf_op | source)
XLA Modules:
  0.0 729.3 jit_solution(1402167555871297250)
XLA Ops:
  7.2 1.8 fusion.71
  9.1 73.1 %all-gather.11.cloned.1.call-done = bf16[1,384,4096]{2,1,0:T(8,128)(2,1)} async-done(((bf16[1,24,4096]{2,1,0:T(8,128)(2,1)}), bf16[1,384,4096]{2,1,0:T(8,128)(2,1)}) %all-gather.11.cloned.1.call-update) | async-done | bytes 3145744 | tf_op jit(solution)/shard_map/all_gather | solution.py:17
  82.2 6.9 fusion.37
  89.2 17.1 %all-reduce.5.cloned.1.call-done = bf16[384,512]{1,0:T(8,128)(2,1)} async-done(((bf16[384,512]{1,0:T(8,128)(2,1)}), bf16[384,512]{1,0:T(8,128)(2,1)}) %all-reduce.5.cloned.1.call-update) | async-done | bytes 393232 | tf_op jit(solution)/shard_map/psum | solution.py:28
  106.3 8.1 %convolution_multiply_fusion.1 = f32[384,4096]{1,0:T(8,128)} fusion(f32[4096,512]{1,0:T(8,128)} %param.10, bf16[384,512]{1,0:T(8,128)(2,1)} %all-reduce.5.cloned.1.call-done), kind=kOutput, calls=%fused_computation.9 | convolution fusion | flops 1614675968 | bytes 15073280 | tf_op jit(solution)/shard_map/dot_general | solution.py:32
  114.4 147.1 %reduce-scatter.3.cloned.1.call-done = f32[24,4096]{1,0:T(8,128)} async-done(((f32[384,4096]{1,0:T(8,128)}), f32[24,4096]{1,0:T(8,128)}) %reduce-scatter.3.cloned.1.call-update) | async-done | bytes 393232 | tf_op jit(solution)/shard_map/reduce_scatter | solution.py:31
  261.5 1.8 fusion.60
  263.4 69.0 %all-gather.7.cloned.1.call-done = bf16[384,4096]{1,0:T(8,128)(2,1)} async-done(((bf16[24,4096]{1,0:T(8,128)(2,1)}), bf16[384,4096]{1,0:T(8,128)(2,1)}) %all-gather.7.cloned.1.call-update) | async-done | bytes 3145744 | tf_op jit(solution)/shard_map/all_gather | solution.py:49
  332.4 6.9 fusion.45
  339.3 0.5 all-gather.13.cloned.1.call-update
  339.9 16.5 %all-reduce.7.cloned.1.call-done = bf16[384,512]{1,0:T(8,128)(2,1)} async-done(((bf16[384,512]{1,0:T(8,128)(2,1)}), bf16[384,512]{1,0:T(8,128)(2,1)}) %all-reduce.7.cloned.1.call-update) | async-done | bytes 393232 | tf_op jit(solution)/shard_map/psum | solution.py:56
  356.4 6.8 fusion.7
  363.2 65.8 %all-gather.13.cloned.1.call-done = bf16[1,384,4096]{2,1,0:T(8,128)(2,1)} async-done(((bf16[1,24,4096]{2,1,0:T(8,128)(2,1)}), bf16[1,384,4096]{2,1,0:T(8,128)(2,1)}) %all-gather.13.cloned.1.call-update) | async-done | bytes 3145744 | tf_op jit(solution)/shard_map/all_gather | solution.py:17
  429.0 12.2 %fusion.48 = bf16[384,512]{1,0:T(8,128)(2,1)} fusion(bf16[1,384,4096]{2,1,0:T(8,128)(2,1)} %all-gather.13.cloned.1.call-done, f32[512,4096]{1,0:T(8,128)} %param.8, f32[512,4096]{1,0:T(8,128)} %fusion.7, f32[512,4096]{1,0:T(8,128)} %param.9), kind=kOutput, calls=%fused_computation.34 | convolution fusion | flops 1623588864 | bytes 28704768 | tf_op jit(solution)/shard_map/dot_general | solution.py:20
  441.4 11.2 %multiply_subtract_fusion.2 = (f32[4096,512]{1,0:T(8,128)}, f32[4096,512]{1,0:T(8,128)}) fusion(f32[4096,512]{1,0:T(8,128)} %param.10, f32[4096,512]{1,0:T(8,128)} %param.11, bf16[384,4096]{1,0:T(8,128)(2,1)S(1)} %copy-done.1, bf16[384,512]{1,0:T(8,128)(2,1)S(1)} %copy-done.4), kind=kOutput, calls=%fused_computation.4 | convolution fusion | flops 1621491712 | bytes 37093376 | tf_op jit(solution)/shard_map/dot_general | solution.py:50
  452.6 5.7 all-reduce.9.cloned.1.call-done
  458.3 8.1 %convolution_multiply_fusion = f32[384,4096]{1,0:T(8,128)} fusion(f32[4096,512]{1,0:T(8,128)} %get-tuple-element.10, bf16[384,512]{1,0:T(8,128)(2,1)} %all-reduce.9.cloned.1.call-done), kind=kOutput, calls=%fused_computation.8 | convolution fusion | flops 1614675968 | bytes 15073280 | tf_op jit(solution)/shard_map/dot_general | solution.py:32
  466.5 146.6 %reduce-scatter.5.cloned.1.call-done = f32[24,4096]{1,0:T(8,128)} async-done(((f32[384,4096]{1,0:T(8,128)}), f32[24,4096]{1,0:T(8,128)}) %reduce-scatter.5.cloned.1.call-update) | async-done | bytes 393232 | tf_op jit(solution)/shard_map/reduce_scatter | solution.py:31
  613.1 1.8 fusion.57
  615.0 69.2 %all-gather.9.cloned.1.call-done = bf16[384,4096]{1,0:T(8,128)(2,1)} async-done(((bf16[24,4096]{1,0:T(8,128)(2,1)}), bf16[384,4096]{1,0:T(8,128)(2,1)}) %all-gather.9.cloned.1.call-update) | async-done | bytes 3145744 | tf_op jit(solution)/shard_map/all_gather | solution.py:49
  684.2 6.9 fusion.42
  691.1 14.7 %multiply_subtract_fusion = (f32[4096,512]{1,0:T(8,128)}, f32[4096,512]{1,0:T(8,128)}) fusion(f32[4096,512]{1,0:T(8,128)} %get-tuple-element.10, f32[4096,512]{1,0:T(8,128)} %param.11, f32[4096,512]{1,0:T(8,128)} %get-tuple-element.11, bf16[384,4096]{1,0:T(8,128)(2,1)} %all-gather.9.cloned.1.call-done, bf16[384,512]{1,0:T(8,128)(2,1)S(1)} %copy-done.3), kind=kOutput, calls=%fused_computation | convolution fusion | flops 1625686016 | bytes 45481984 | tf_op jit(solution)/shard_map/dot_general | solution.py:50
  705.8 2.4 all-reduce.11.cloned.1.call-done
  708.2 14.2 %multiply_subtract_fusion.1 = (f32[512,4096]{1,0:T(8,128)}, f32[512,4096]{1,0:T(8,128)}) fusion(f32[512,4096]{1,0:T(8,128)} %param.8, f32[512,4096]{1,0:T(8,128)} %param.9, f32[512,4096]{1,0:T(8,128)} %fusion.7, bf16[1,384,4096]{2,1,0:T(8,128)(2,1)S(1)} %copy-done, bf16[384,512]{1,0:T(8,128)(2,1)} %all-reduce.11.cloned.1.call-done, ...), kind=kOutput, calls=%fused_computation.2 | convolution fusion | flops 1632763904 | bytes 45875200 | tf_op jit(solution)/shard_map/dot_general | solution.py:58
  (31 shorter events, 0.8 us)
Async XLA Ops:
  7.2 75.1 %all-gather.11.cloned.1.call-start = ((), (), s32[]{:S(2)}) async-start(), calls=%async_computation.10 | async-start | bytes 3342336 | tf_op jit(solution)/shard_map/all_gather | solution.py:17
  9.0 97.3 %all-reduce.5.cloned.1.call-start = ((), (), s32[]{:S(2)}) async-start(), calls=%async_computation.2 | async-start | bytes 786432 | tf_op jit(solution)/shard_map/psum | solution.py:28
  89.2 172.4 %reduce-scatter.3.cloned.1.call-start = ((), (), s32[]{:S(2)}) async-start(), calls=%async_computation.3 | async-start | bytes 6684672 | tf_op jit(solution)/shard_map/reduce_scatter | solution.py:31
  114.4 242.1 %copy-start.2 = (bf16[1,384,4096]{2,1,0:T(8,128)(2,1)S(1)}, bf16[1,384,4096]{2,1,0:T(8,128)(2,1)}, u32[]{:S(2)}) copy-start(bf16[1,384,4096]{2,1,0:T(8,128)(2,1)} %all-gather.11.cloned.1.call-done) | copy-start | bytes 9437188
  114.4 242.1 %copy-start.4 = (bf16[384,512]{1,0:T(8,128)(2,1)S(1)}, bf16[384,512]{1,0:T(8,128)(2,1)}, u32[]{:S(2)}) copy-start(bf16[384,512]{1,0:T(8,128)(2,1)} %all-reduce.5.cloned.1.call-done) | copy-start | bytes 1179652
  114.4 218.0 %all-gather.7.cloned.1.call-start = ((), (), s32[]{:S(2)}) async-start(), calls=%async_computation.4 | async-start | bytes 3342336 | tf_op jit(solution)/shard_map/all_gather | solution.py:49
  263.4 93.0 %all-reduce.7.cloned.1.call-start = ((), (), s32[]{:S(2)}) async-start(), calls=%async_computation.5 | async-start | bytes 786432 | tf_op jit(solution)/shard_map/psum | solution.py:56
  339.3 89.7 %all-gather.13.cloned.1.call-start = ((), (), s32[]{:S(2)}) async-start(), calls=%async_computation.11 | async-start | bytes 3342336 | tf_op jit(solution)/shard_map/all_gather | solution.py:17
  339.9 118.5 %all-reduce.9.cloned.1.call-start = ((), (), s32[]{:S(2)}) async-start(), calls=%async_computation.6 | async-start | bytes 786432 | tf_op jit(solution)/shard_map/psum | solution.py:28
  363.2 78.2 %copy-start.1 = (bf16[384,4096]{1,0:T(8,128)(2,1)S(1)}, bf16[384,4096]{1,0:T(8,128)(2,1)}, u32[]{:S(2)}) copy-start(bf16[384,4096]{1,0:T(8,128)(2,1)} %all-gather.7.cloned.1.call-done) | copy-start | bytes 9437188
  441.2 171.9 %reduce-scatter.5.cloned.1.call-start = ((), (), s32[]{:S(2)}) async-start(), calls=%async_computation.7 | async-start | bytes 6684672 | tf_op jit(solution)/shard_map/reduce_scatter | solution.py:31
  458.3 154.8 %copy-start.5 = (bf16[2,24,4096]{2,1,0:T(8,128)(2,1)S(1)}, bf16[2,24,4096]{2,1,0:T(8,128)(2,1)}, u32[]{:S(2)}) copy-start(bf16[2,24,4096]{2,1,0:T(8,128)(2,1)} %param.7) | copy-start | bytes 1179652
  466.4 224.6 %copy-start.3 = (bf16[384,512]{1,0:T(8,128)(2,1)S(1)}, bf16[384,512]{1,0:T(8,128)(2,1)}, u32[]{:S(2)}) copy-start(bf16[384,512]{1,0:T(8,128)(2,1)} %all-reduce.9.cloned.1.call-done) | copy-start | bytes 1179652
  466.5 217.7 %all-gather.9.cloned.1.call-start = ((), (), s32[]{:S(2)}) async-start(), calls=%async_computation.8 | async-start | bytes 3342336 | tf_op jit(solution)/shard_map/all_gather | solution.py:49
  614.9 93.3 %all-reduce.11.cloned.1.call-start = ((), (), s32[]{:S(2)}) async-start(), calls=%async_computation.9 | async-start | bytes 786432 | tf_op jit(solution)/shard_map/psum | solution.py:56
  691.1 17.1 %copy-start = (bf16[1,384,4096]{2,1,0:T(8,128)(2,1)S(1)}, bf16[1,384,4096]{2,1,0:T(8,128)(2,1)}, u32[]{:S(2)}) copy-start(bf16[1,384,4096]{2,1,0:T(8,128)(2,1)} %all-gather.13.cloned.1.call-done) | copy-start | bytes 9437188
Sparse Core Ops, SparseCore 0:
  11.3 70.8 all-gather.10
  89.3 16.9 all-reduce.4
  114.5 146.9 reduce-scatter.2
  265.1 67.2 all-gather.6
  339.4 16.9 all-reduce.6
  359.6 69.3 all-gather.12
  441.3 16.9 all-reduce.8
  466.6 146.4 reduce-scatter.4
  616.8 67.2 all-gather.8
  691.2 16.9 all-reduce.10
where the time goes:
time: 730 us; the launch traced here: 729 us
  waiting for transfers between devices  613 us (84%)
  matrix products  96 us (13%)
  between operations  14.2 us (2%)
    reduce_scatter x2, waiting for transfers between devices, local(): lax.psum_scatter(lax.dot_general(first_rows, second_half, (((1,), (1,)),...  294 us
    all_gather x2, waiting for transfers between devices, local(): lax.all_gather(inputs[round_index], 'replica', axis=0, tiled=True)  139 us
    all_gather x2, waiting for transfers between devices, local(): error_half = lax.all_gather(error_own, 'replica', axis=0, tiled=True)  138 us
    dot_general x2, matrix products, local(): lax.dot_general(error_half, first_rows, (((0,), (0,)), ((), ())), preferr...  25.9 us
    psum x2, waiting for transfers between devices, local(): lax.psum(first_terms.astype(jnp.bfloat16), 'dom').astype(jnp.float32)  22.8 us
    dot_general x2, matrix products, local(): lax.dot_general(first_error, round_batch, (((0,), (0,)), ((), ())), prefe...  21 us
    dot_general x2, matrix products, local(): lax.dot_general(round_batch, first_half, (((1,), (1,)), ((), ())), prefer...  19.1 us
    psum x2, waiting for transfers between devices, local(): lax.psum(back_terms.astype(jnp.bfloat16), 'dom').astype(jnp.float32)  18.9 us
  transfers between devices with their start and end apart: 10, of which 10 were waited for; matrix products, arithmetic and copies ran while one was open for 4% of the time, Pallas kernels for 0%

commit v1 on v0

--- a/solution.py
+++ b/solution.py
@@ -6,6 +6,18 @@
 
 learn_rate = 0.05
 error_weight = 0.25
+
+
+def gather_by_bits(shard, axis, dim):
+    ways, here = (lax.axis_size(axis), lax.axis_index(axis))
+    grown, reach = (shard, 1)
+    while reach < ways:
+        theirs = lax.ppermute(grown, axis, [(d, d ^ reach) for d in range(ways)])
+        mine_first = jnp.concatenate([grown, theirs], axis=dim)
+        theirs_first = jnp.concatenate([theirs, grown], axis=dim)
+        grown = jnp.where(here & reach == 0, mine_first, theirs_first)
+        reach = 2 * reach
+    return grown
 
 
 def local(inputs, targets, w_first, acc_first, w_second, acc_second):
@@ -46,7 +58,7 @@
             * error_weight
             * (1.0 - second_out * second_out)
         ).astype(jnp.bfloat16)
-        error_half = lax.all_gather(error_own, "replica", axis=0, tiled=True)
+        error_half = gather_by_bits(error_own, "replica", 0)
         second_grad = lax.dot_general(
             error_half, first_rows, (((0,), (0,)), ((), ())), preferred_element_type=jnp.float32
         )

time: 730 us -> 789 us (1.081)
  waiting for transfers between devices: 613 us -> 654 us
  starting transfers between devices: 0.59 us -> 10.1 us
    ppermute x0 -> x8, waiting for transfers between devices: none -> 184 us  [gather_by_bits(): theirs = lax.ppermute(grown, axis, [(d, d ^ reach) for d in range(ways)])]
    all_gather x2 -> x0, waiting for transfers between devices: 138 us -> none  [local(): error_half = lax.all_gather(error_own, 'replica', axis=0, tiled=True)]
    ppermute x0 -> x8, starting transfers between devices: none -> 9.55 us  [gather_by_bits(): theirs = lax.ppermute(grown, axis, [(d, d ^ reach) for d in range(ways)])]
  transfers between devices with their start and end apart: 10 -> 16, of which waited for: 10 -> 15; matrix products, arithmetic and copies ran while one was open for 4% -> 5% of each run, Pallas kernels for 0% -> 0%
where the time goes in v1:
time: 789 us
  waiting for transfers between devices  654 us (83%)
  matrix products  103 us (13%)
  between operations  14.2 us (2%)
  starting transfers between devices  10.1 us (1%)
    reduce_scatter x2, waiting for transfers between devices, local(): lax.psum_scatter(lax.dot_general(first_rows, second_half, (((1,), (1,)),...  294 us
    ppermute x8, waiting for transfers between devices, gather_by_bits(): theirs = lax.ppermute(grown, axis, [(d, d ^ reach) for d in range(ways)])  184 us
    all_gather x2, waiting for transfers between devices, local(): lax.all_gather(inputs[round_index], 'replica', axis=0, tiled=True)  139 us
    dot_general x2, matrix products, local(): lax.dot_general(error_half, first_rows, (((0,), (0,)), ((), ())), preferr...  33.1 us
    dot_general x2, matrix products, local(): lax.dot_general(first_error, round_batch, (((0,), (0,)), ((), ())), prefe...  21 us
    psum x2, waiting for transfers between devices, local(): lax.psum(first_terms.astype(jnp.bfloat16), 'dom').astype(jnp.float32)  19.8 us
    dot_general x2, matrix products, local(): lax.dot_general(round_batch, first_half, (((1,), (1,)), ((), ())), prefer...  19.1 us
    psum x2, waiting for transfers between devices, local(): lax.psum(back_terms.astype(jnp.bfloat16), 'dom').astype(jnp.float32)  17.1 us
  transfers between devices with their start and end apart: 16, of which 15 were waited for; matrix products, arithmetic and copies ran while one was open for 5% of the time, Pallas kernels for 0%

profile of v1, /device:TPU:0, one launch (start us, length us, event | category | flops | bytes accessed | tf_op | source)
XLA Modules:
  0.0 789.0 jit_solution(5411567100600536380)
XLA Ops:
  9.1 73.1 %all-gather.5.cloned.1.call-done = bf16[1,384,4096]{2,1,0:T(8,128)(2,1)} async-done(((bf16[1,24,4096]{2,1,0:T(8,128)(2,1)}), bf16[1,384,4096]{2,1,0:T(8,128)(2,1)}) %all-gather.5.cloned.1.call-update) | async-done | bytes 3145744 | tf_op jit(solution)/shard_map/all_gather | solution.py:29
  82.2 6.9 fusion.37
  89.2 17.1 %all-reduce.5.cloned.1.call-done = bf16[384,512]{1,0:T(8,128)(2,1)} async-done(((bf16[384,512]{1,0:T(8,128)(2,1)}), bf16[384,512]{1,0:T(8,128)(2,1)}) %all-reduce.5.cloned.1.call-update) | async-done | bytes 393232 | tf_op jit(solution)/shard_map/psum | solution.py:40
  106.3 8.1 %convolution_multiply_fusion.1 = f32[384,4096]{1,0:T(8,128)} fusion(f32[4096,512]{1,0:T(8,128)} %param.10, bf16[384,512]{1,0:T(8,128)(2,1)} %all-reduce.5.cloned.1.call-done), kind=kOutput, calls=%fused_computation.9 | convolution fusion | flops 1614675968 | bytes 15073280 | tf_op jit(solution)/shard_map/dot_general | solution.py:44
  114.4 147.1 %reduce-scatter.3.cloned.1.call-done = f32[24,4096]{1,0:T(8,128)} async-done(((f32[384,4096]{1,0:T(8,128)}), f32[24,4096]{1,0:T(8,128)}) %reduce-scatter.3.cloned.1.call-update) | async-done | bytes 393232 | tf_op jit(solution)/shard_map/reduce_scatter | solution.py:43
  264.1 4.3 collective-permute-done
  270.0 7.0 collective-permute-done.1
  278.0 15.2 %collective-permute-done.2 = bf16[96,4096]{1,0:T(8,128)(2,1)S(1)} collective-permute-done((bf16[96,4096]{1,0:T(8,128)(2,1)S(1)}, bf16[96,4096]{1,0:T(8,128)(2,1)S(1)}, u32[]{:S(2)}, u32[]{:S(2)}) %collective-permute-start.2) | collective-permute-done | bytes 786464 | tf_op jit(solution)/shard_map/ppermute | solution.py:15
  295.4 65.6 %collective-permute-done.3 = bf16[192,4096]{1,0:T(8,128)(2,1)} collective-permute-done((bf16[192,4096]{1,0:T(8,128)(2,1)}, bf16[192,4096]{1,0:T(8,128)(2,1)}, u32[]{:S(2)}, u32[]{:S(2)}) %collective-permute-start.3) | collective-permute-done | bytes 1572896 | tf_op jit(solution)/shard_map/ppermute | solution.py:15
  361.0 7.8 fusion.45
  369.5 17.1 %all-reduce.7.cloned.1.call-done = bf16[384,512]{1,0:T(8,128)(2,1)} async-done(((bf16[384,512]{1,0:T(8,128)(2,1)}), bf16[384,512]{1,0:T(8,128)(2,1)}) %all-reduce.7.cloned.1.call-update) | async-done | bytes 393232 | tf_op jit(solution)/shard_map/psum | solution.py:68
  386.6 6.8 fusion.7
  393.4 65.8 %all-gather.7.cloned.1.call-done = bf16[1,384,4096]{2,1,0:T(8,128)(2,1)} async-done(((bf16[1,24,4096]{2,1,0:T(8,128)(2,1)}), bf16[1,384,4096]{2,1,0:T(8,128)(2,1)}) %all-gather.7.cloned.1.call-update) | async-done | bytes 3145744 | tf_op jit(solution)/shard_map/all_gather | solution.py:29
  459.2 12.2 %fusion.48 = bf16[384,512]{1,0:T(8,128)(2,1)} fusion(bf16[1,384,4096]{2,1,0:T(8,128)(2,1)} %all-gather.7.cloned.1.call-done, f32[512,4096]{1,0:T(8,128)} %param.8, f32[512,4096]{1,0:T(8,128)} %fusion.7, f32[512,4096]{1,0:T(8,128)} %param.9), kind=kOutput, calls=%fused_computation.38 | convolution fusion | flops 1623588864 | bytes 28704768 | tf_op jit(solution)/shard_map/dot_general | solution.py:32
  471.7 14.2 %multiply_subtract_fusion.2 = (f32[4096,512]{1,0:T(8,128)}, f32[4096,512]{1,0:T(8,128)}) fusion(f32[4096,512]{1,0:T(8,128)} %param.10, f32[4096,512]{1,0:T(8,128)} %param.11, bf16[384,512]{1,0:T(8,128)(2,1)S(1)} %copy-done.4, bf16[192,4096]{1,0:T(8,128)(2,1)} %collective-permute-done.3, bf16[192,4096]{1,0:T(8,128)(2,1)} %maximum_select_fusion.2, pred[]{:T(512)S(6)} %eq.16), kind=kOutput, calls=%fused_computation.4 | convolution fusion | flops 1635647488 | bytes 37093376 | tf_op jit(solution)/shard_map/dot_general | solution.py:62
  488.6 8.1 %convolution_multiply_fusion = f32[384,4096]{1,0:T(8,128)} fusion(f32[4096,512]{1,0:T(8,128)} %get-tuple-element.10, bf16[384,512]{1,0:T(8,128)(2,1)} %all-reduce.9.cloned.1.call-done), kind=kOutput, calls=%fused_computation.8 | convolution fusion | flops 1614675968 | bytes 15073280 | tf_op jit(solution)/shard_map/dot_general | solution.py:44
  496.7 146.6 %reduce-scatter.5.cloned.1.call-done = f32[24,4096]{1,0:T(8,128)} async-done(((f32[384,4096]{1,0:T(8,128)}), f32[24,4096]{1,0:T(8,128)}) %reduce-scatter.5.cloned.1.call-update) | async-done | bytes 393232 | tf_op jit(solution)/shard_map/reduce_scatter | solution.py:43
  645.9 4.2 collective-permute-done.4
  651.8 7.0 collective-permute-done.5
  659.9 16.0 %collective-permute-done.6 = bf16[96,4096]{1,0:T(8,128)(2,1)S(1)} collective-permute-done((bf16[96,4096]{1,0:T(8,128)(2,1)S(1)}, bf16[96,4096]{1,0:T(8,128)(2,1)S(1)}, u32[]{:S(2)}, u32[]{:S(2)}) %collective-permute-start.6) | collective-permute-done | bytes 786464 | tf_op jit(solution)/shard_map/ppermute | solution.py:15
  677.1 64.8 %collective-permute-done.7 = bf16[192,4096]{1,0:T(8,128)(2,1)S(1)} collective-permute-done((bf16[192,4096]{1,0:T(8,128)(2,1)S(1)}, bf16[192,4096]{1,0:T(8,128)(2,1)S(1)}, u32[]{:S(2)}, u32[]{:S(2)}) %collective-permute-start.7) | collective-permute-done | bytes 1572896 | tf_op jit(solution)/shard_map/ppermute | solution.py:15
  743.0 6.0 fusion.42
  749.1 18.8 %multiply_subtract_fusion = (f32[4096,512]{1,0:T(8,128)}, f32[4096,512]{1,0:T(8,128)}) fusion(f32[4096,512]{1,0:T(8,128)} %get-tuple-element.10, f32[4096,512]{1,0:T(8,128)} %param.11, f32[4096,512]{1,0:T(8,128)} %get-tuple-element.11, bf16[384,512]{1,0:T(8,128)(2,1)S(1)} %copy-done.3, bf16[192,4096]{1,0:T(8,128)(2,1)} %copy-done.5, ...), kind=kOutput, calls=%fused_computation | convolution fusion | flops 1639841792 | bytes 45481984 | tf_op jit(solution)/shard_map/dot_general | solution.py:62
  767.9 14.3 %multiply_subtract_fusion.1 = (f32[512,4096]{1,0:T(8,128)}, f32[512,4096]{1,0:T(8,128)}) fusion(f32[512,4096]{1,0:T(8,128)} %param.8, f32[512,4096]{1,0:T(8,128)} %param.9, f32[512,4096]{1,0:T(8,128)} %fusion.7, bf16[1,384,4096]{2,1,0:T(8,128)(2,1)S(1)} %copy-done, bf16[384,512]{1,0:T(8,128)(2,1)} %all-reduce.11.cloned.1.call-done, ...), kind=kOutput, calls=%fused_computation.2 | convolution fusion | flops 1632763904 | bytes 45875200 | tf_op jit(solution)/shard_map/dot_general | solution.py:70
  (51 shorter events, 20.8 us)
Async XLA Ops:
  7.2 75.1 %all-gather.5.cloned.1.call-start = ((), (), s32[]{:S(2)}) async-start(), calls=%async_computation.8 | async-start | bytes 3342336 | tf_op jit(solution)/shard_map/all_gather | solution.py:29
  9.0 97.3 %all-reduce.5.cloned.1.call-start = ((), (), s32[]{:S(2)}) async-start(), calls=%async_computation.2 | async-start | bytes 786432 | tf_op jit(solution)/shard_map/psum | solution.py:40
  89.2 172.4 %reduce-scatter.3.cloned.1.call-start = ((), (), s32[]{:S(2)}) async-start(), calls=%async_computation.3 | async-start | bytes 6684672 | tf_op jit(solution)/shard_map/reduce_scatter | solution.py:43
  114.4 147.2 %copy-start.6 = (bf16[2,24,4096]{2,1,0:T(8,128)(2,1)S(1)}, bf16[2,24,4096]{2,1,0:T(8,128)(2,1)}, u32[]{:S(2)}) copy-start(bf16[2,24,4096]{2,1,0:T(8,128)(2,1)} %param.7) | copy-start | bytes 1179652
  114.4 272.2 %all-reduce.7.cloned.1.call-start = ((), (), s32[]{:S(2)}) async-start(), calls=%async_computation.4 | async-start | bytes 786432 | tf_op jit(solution)/shard_map/psum | solution.py:68
  262.6 5.7 collective-permute-start
  268.4 8.5 %collective-permute-start.1 = (bf16[48,4096]{1,0:T(8,128)(2,1)S(1)}, bf16[48,4096]{1,0:T(8,128)(2,1)S(1)}, u32[]{:S(2)}, u32[]{:S(2)}) collective-permute-start(bf16[48,4096]{1,0:T(8,128)(2,1)S(1)} %maximum_select_fusion.10), channel_id=1, source_target_pairs={{0,4},{2,6},{4,0},{6,2},{8,12},{10,14},{12,8},{14,10},{16,20},{18,... | collective-permute-start | bytes 1179656 | tf_op jit(solution)/shard_map/ppermute | solution.py:15
  277.1 16.0 %collective-permute-start.2 = (bf16[96,4096]{1,0:T(8,128)(2,1)S(1)}, bf16[96,4096]{1,0:T(8,128)(2,1)S(1)}, u32[]{:S(2)}, u32[]{:S(2)}) collective-permute-start(bf16[96,4096]{1,0:T(8,128)(2,1)S(1)} %maximum_select_fusion.4), channel_id=1, source_target_pairs={{0,8},{2,10},{4,12},{6,14},{8,0},{10,2},{12,4},{14,6},{16,24},{18,... | collective-permute-start | bytes 2359304 | tf_op jit(solution)/shard_map/ppermute | solution.py:15
  294.6 66.4 %collective-permute-start.3 = (bf16[192,4096]{1,0:T(8,128)(2,1)}, bf16[192,4096]{1,0:T(8,128)(2,1)}, u32[]{:S(2)}, u32[]{:S(2)}) collective-permute-start(bf16[192,4096]{1,0:T(8,128)(2,1)} %maximum_select_fusion.2), channel_id=1, source_target_pairs={{0,16},{2,18},{4,20},{6,22},{8,24},{10,26},{12,28},{14,30},{16,0},... | collective-permute-start | bytes 4718600 | tf_op jit(solution)/shard_map/ppermute | solution.py:15
  295.4 91.2 %copy-start.1 = (bf16[1,384,4096]{2,1,0:T(8,128)(2,1)S(1)}, bf16[1,384,4096]{2,1,0:T(8,128)(2,1)}, u32[]{:S(2)}) copy-start(bf16[1,384,4096]{2,1,0:T(8,128)(2,1)} %all-gather.5.cloned.1.call-done) | copy-start | bytes 9437188
  295.4 91.2 %copy-start.4 = (bf16[384,512]{1,0:T(8,128)(2,1)S(1)}, bf16[384,512]{1,0:T(8,128)(2,1)}, u32[]{:S(2)}) copy-start(bf16[384,512]{1,0:T(8,128)(2,1)} %all-reduce.5.cloned.1.call-done) | copy-start | bytes 1179652
  368.9 90.3 %all-gather.7.cloned.1.call-start = ((), (), s32[]{:S(2)}) async-start(), calls=%async_computation.9 | async-start | bytes 3342336 | tf_op jit(solution)/shard_map/all_gather | solution.py:29
  369.5 119.1 %all-reduce.9.cloned.1.call-start = ((), (), s32[]{:S(2)}) async-start(), calls=%async_computation.5 | async-start | bytes 786432 | tf_op jit(solution)/shard_map/psum | solution.py:40
  471.4 171.9 %reduce-scatter.5.cloned.1.call-start = ((), (), s32[]{:S(2)}) async-start(), calls=%async_computation.6 | async-start | bytes 6684672 | tf_op jit(solution)/shard_map/reduce_scatter | solution.py:43
  496.6 146.7 %copy-start.7 = (bf16[2,24,4096]{2,1,0:T(8,128)(2,1)S(1)}, bf16[2,24,4096]{2,1,0:T(8,128)(2,1)}, u32[]{:S(2)}) copy-start(bf16[2,24,4096]{2,1,0:T(8,128)(2,1)} %param.7) | copy-start | bytes 1179652
  496.6 271.3 %all-reduce.11.cloned.1.call-start = ((), (), s32[]{:S(2)}) async-start(), calls=%async_computation.7 | async-start | bytes 786432 | tf_op jit(solution)/shard_map/psum | solution.py:68
  644.4 5.7 collective-permute-start.4
  650.2 8.5 %collective-permute-start.5 = (bf16[48,4096]{1,0:T(8,128)(2,1)S(1)}, bf16[48,4096]{1,0:T(8,128)(2,1)S(1)}, u32[]{:S(2)}, u32[]{:S(2)}) collective-permute-start(bf16[48,4096]{1,0:T(8,128)(2,1)S(1)} %maximum_select_fusion.11), channel_id=1, source_target_pairs={{0,4},{2,6},{4,0},{6,2},{8,12},{10,14},{12,8},{14,10},{16,20},{18,... | collective-permute-start | bytes 1179656 | tf_op jit(solution)/shard_map/ppermute | solution.py:15
  658.9 16.9 %collective-permute-start.6 = (bf16[96,4096]{1,0:T(8,128)(2,1)S(1)}, bf16[96,4096]{1,0:T(8,128)(2,1)S(1)}, u32[]{:S(2)}, u32[]{:S(2)}) collective-permute-start(bf16[96,4096]{1,0:T(8,128)(2,1)S(1)} %maximum_select_fusion.5), channel_id=1, source_target_pairs={{0,8},{2,10},{4,12},{6,14},{8,0},{10,2},{12,4},{14,6},{16,24},{18,... | collective-permute-start | bytes 2359304 | tf_op jit(solution)/shard_map/ppermute | solution.py:15
  676.2 65.7 %copy-start.2 = (bf16[192,4096]{1,0:T(8,128)(2,1)}, bf16[192,4096]{1,0:T(8,128)(2,1)S(1)}, u32[]{:S(2)}) copy-start(bf16[192,4096]{1,0:T(8,128)(2,1)S(1)} %maximum_select_fusion.3) | copy-start | bytes 4718596
  676.2 72.9 %copy-start.3 = (bf16[384,512]{1,0:T(8,128)(2,1)S(1)}, bf16[384,512]{1,0:T(8,128)(2,1)}, u32[]{:S(2)}) copy-start(bf16[384,512]{1,0:T(8,128)(2,1)} %all-reduce.9.cloned.1.call-done) | copy-start | bytes 1179652
  676.2 65.7 %collective-permute-start.7 = (bf16[192,4096]{1,0:T(8,128)(2,1)S(1)}, bf16[192,4096]{1,0:T(8,128)(2,1)S(1)}, u32[]{:S(2)}, u32[]{:S(2)}) collective-permute-start(bf16[192,4096]{1,0:T(8,128)(2,1)S(1)} %maximum_select_fusion.3), channel_id=1, source_target_pairs={{0,16},{2,18},{4,20},{6,22},{8,24},{10,26},{12,28},{14,30},{16,0},... | collective-permute-start | bytes 4718600 | tf_op jit(solution)/shard_map/ppermute | solution.py:15
  741.9 1.1 copy-start.5
  749.1 18.9 %copy-start = (bf16[1,384,4096]{2,1,0:T(8,128)(2,1)S(1)}, bf16[1,384,4096]{2,1,0:T(8,128)(2,1)}, u32[]{:S(2)}) copy-start(bf16[1,384,4096]{2,1,0:T(8,128)(2,1)} %all-gather.7.cloned.1.call-done) | copy-start | bytes 9437188
Sparse Core Ops, SparseCore 0:
  11.3 70.8 all-gather.4
  89.3 16.9 all-reduce.4
  114.5 146.9 reduce-scatter.2
  369.0 17.5 all-reduce.6
  389.8 69.3 all-gather.6
  471.6 16.9 all-reduce.8
  496.8 146.4 reduce-scatter.4
  749.2 17.5 all-reduce.10
